TPU v7x, 256 devices: a whole 4x4x8 slice. The times are simulated.
256 devices in a mesh: section: 2 (over y_hi), segment: 8 (over x, core), fsdp: 16 (over z, y_lo).
Axes of the slice: x: 4, y: 4 (y_hi: 2, y_lo: 2; y = y_hi * 2 + y_lo), z: 8, core: 2. Of those that a mesh axis runs over, the one named last changes fastest.
Arguments:
- out_grad: bfloat16 [2, 16, 256, 6144], P(None, 'fsdp'), may hold values from -48 to 48
- queries: bfloat16 [2, 16, 256, 6144], P(None, 'fsdp', None, 'segment'), may hold values from -40 to 40
- enc_keys: bfloat16 [2, 16, 256, 6144], P(None, 'fsdp', None, 'segment'), may hold values from -4 to 4
- enc_values: bfloat16 [2, 16, 256, 6144], P(None, 'fsdp', None, 'segment'), may hold values from -6 to 6
- key_mask: int32 [2, 16, 256], P(None, 'fsdp'), may hold values from 0 to 1, as said below
- weights: bfloat16 [2, 2, 6144, 6144], P('section', None, 'fsdp', 'segment'), may hold values from -0.078125 to 0.078125
Outputs:
- grads: bfloat16 [2, 2, 16, 256, 6144], P('section', None, 'fsdp', None, 'segment')
Inputs may be any that keep to these rules, and one draw needn't show every extreme that they name: `key_mask`: each row is 1 on a prefix of 128 or more positions and 0 after it; the first reaction of every microbatch has no padding.
All inputs are finite; a program needn't handle non-finite values.
Results may differ from a plain program's by a relative error of at most 0.014.
Values may be sent and summed in bfloat16 or wider, within the bound.
No kernel may reach another device: no remote copies, remote signals or barrier semaphores. Data moves between devices by JAX's collectives and lax.ppermute only.
A program may use at most 128 MiB of HBM per device.

v0:
```python
import jax
import jax.numpy as jnp
from jax import lax
from jax.sharding import PartitionSpec as P

HDIM = 128


def passed_along(value, axis, by):
    peers = lax.axis_size(axis)
    pairs = [(i, i + by) for i in range(peers) if 0 <= i + by < peers]
    return lax.ppermute(value, axis, pairs)


def attend(grad_rows, first_weight, queries, enc_keys, enc_values, key_mask):
    reaction_count, seq_length, local_width = queries.shape
    head_count = local_width // HDIM
    score_scale = HDIM ** (-0.5)
    ctx_grad = jnp.dot(grad_rows, first_weight, preferred_element_type=jnp.float32).astype(
        jnp.bfloat16
    )
    shaped = (reaction_count, seq_length, head_count, HDIM)
    grad_heads = ctx_grad.reshape(shaped)
    query_heads = queries.reshape(shaped)
    key_heads = enc_keys.reshape(shaped)
    value_heads = enc_values.reshape(shaped)
    scores = (
        jnp.einsum("bihc,bjhc->bhij", query_heads, key_heads, preferred_element_type=jnp.float32)
        * score_scale
    )
    scores = jnp.where(key_mask[:, None, None, :] > 0, scores, -jnp.inf)
    row_top = jnp.max(scores, axis=-1, keepdims=True)
    exp_scores = jnp.exp(scores - row_top)
    probabilities = exp_scores / jnp.sum(exp_scores, axis=-1, keepdims=True)
    probs_half = probabilities.astype(jnp.bfloat16)
    prob_grad = jnp.einsum(
        "bihc,bjhc->bhij", grad_heads, value_heads, preferred_element_type=jnp.float32
    )
    center = jnp.sum(probabilities * prob_grad, axis=-1, keepdims=True)
    score_grad = (probabilities * (prob_grad - center)).astype(jnp.bfloat16)
    query_grad = (
        jnp.einsum("bhij,bjhc->bihc", score_grad, key_heads, preferred_element_type=jnp.float32)
        * score_scale
    ).astype(jnp.bfloat16)
    key_grad = (
        jnp.einsum("bhij,bihc->bjhc", score_grad, query_heads, preferred_element_type=jnp.float32)
        * score_scale
    ).astype(jnp.bfloat16)
    value_grad = jnp.einsum(
        "bhij,bihc->bjhc", probs_half, grad_heads, preferred_element_type=jnp.float32
    ).astype(jnp.bfloat16)
    flat = (reaction_count * seq_length, local_width)
    return (query_grad.reshape(flat), key_grad.reshape(flat), value_grad.reshape(flat))


def project(grad_rows, weight_cols):
    return lax.dot_general(
        grad_rows, weight_cols, (((1,), (1,)), ((), ())), preferred_element_type=jnp.float32
    )


def per_device(out_grad, queries, enc_keys, enc_values, key_mask, weights):
    decoder = lax.axis_index("section") == 1
    gathered = lax.all_gather(weights, "fsdp", axis=2, tiled=True)
    first_weight = gathered[0, 0]
    second_weight = gathered[0, 1]
    micro_count, reaction_count, seq_length, feature_width = out_grad.shape
    local_width = queries.shape[3]
    row_count = micro_count * reaction_count * seq_length
    flat = (micro_count * reaction_count, seq_length, local_width)

    def decoder_work():
        return attend(
            out_grad.reshape(row_count, feature_width),
            first_weight,
            queries.reshape(flat),
            enc_keys.reshape(flat),
            enc_values.reshape(flat),
            key_mask.reshape(micro_count * reaction_count, seq_length),
        )

    def encoder_work():
        blank_grads = jnp.zeros((row_count, local_width), jnp.bfloat16)
        return (blank_grads, blank_grads, blank_grads)

    query_grad, key_grad, value_grad = lax.cond(decoder, decoder_work, encoder_work)
    got_keys, got_values = passed_along((key_grad, value_grad), "section", -1)
    partial_sum = lax.cond(
        decoder,
        lambda: project(query_grad, second_weight),
        lambda: project(got_keys, first_weight) + project(got_values, second_weight),
    )
    summed = lax.psum_scatter(
        partial_sum.astype(jnp.bfloat16), "segment", scatter_dimension=1, tiled=True
    ).astype(jnp.float32)
    result = summed.astype(jnp.bfloat16).reshape(
        1, micro_count, reaction_count, seq_length, summed.shape[1]
    )
    return result


def solution(mesh):
    return jax.shard_map(
        per_device,
        mesh=mesh,
        in_specs=(
            P(None, "fsdp", None, None),
            P(None, "fsdp", None, "segment"),
            P(None, "fsdp", None, "segment"),
            P(None, "fsdp", None, "segment"),
            P(None, "fsdp", None),
            P("section", None, "fsdp", "segment"),
        ),
        out_specs=P("section", None, "fsdp", None, "segment"),
        check_vma=False,
    )
```

profile of v0, /device:TPU:1, one launch (start us, length us, event | category | flops | bytes accessed | tf_op | source)
XLA Modules:
  0.0 565.3 jit_solution(8359995170980936187)
XLA Ops:
  6.5 0.0 all-gather.2.cloned.1.call-start
  6.5 0.7 all-gather.2.cloned.1.call-update
  7.3 0.0 reduce-scatter.2.cloned.1.call-start
  7.3 0.0 copy-start.3
  7.3 0.0 copy-start.5
  7.3 398.5 %all-gather.2.cloned.1.call-done = bf16[1,2,6144,768]{3,2,1,0:T(8,128)(2,1)} async-done(((bf16[1,2,384,768]{3,2,1,0:T(8,128)(2,1)}), bf16[1,2,6144,768]{3,2,1,0:T(8,128)(2,1)}) %all-gather.2.cloned.1.call-update) | async-done | bytes 18874384 | tf_op jit(solution)/shard_map/all_gather | solution.py:64
  405.9 14.6 %slice_bitcast_fusion = (bf16[6144,768]{1,0:T(8,128)(2,1)}, bf16[6144,768]{1,0:T(8,128)(2,1)}) fusion(bf16[1,2,6144,768]{3,2,1,0:T(8,128)(2,1)} %all-gather.2.cloned.1.call-done), kind=kLoop, calls=%fused_computation.24 | loop fusion | bytes 37748736 | tf_op jit(solution)/shard_map/squeeze | solution.py:66
  420.5 0.0 copy-done.3
  420.5 0.0 copy-done.5
  420.5 1.1 conditional.2
  420.5 0.1 broadcast.21.clone.1
  420.5 0.1 broadcast.21.clone
  420.6 0.9 broadcast.21
  421.5 0.3 copy.39
  421.8 0.3 copy.40
  422.1 1.3 collective-permute-start.1
  423.4 1.3 collective-permute-start
  424.7 43.1 %collective-permute-done.1 = bf16[512,768]{1,0:T(8,128)(2,1)S(1)} collective-permute-done((bf16[512,768]{1,0:T(8,128)(2,1)S(1)}, bf16[512,768]{1,0:T(8,128)(2,1)S(1)}, u32[]{:S(2)}, u32[]{:S(2)}) %collective-permute-start.1) | collective-permute-done | bytes 786464 | tf_op jit(solution)/shard_map/ppermute | solution.py:12
  467.8 16.9 %collective-permute-done = bf16[512,768]{1,0:T(8,128)(2,1)S(1)} collective-permute-done((bf16[512,768]{1,0:T(8,128)(2,1)S(1)}, bf16[512,768]{1,0:T(8,128)(2,1)S(1)}, u32[]{:S(2)}, u32[]{:S(2)}) %collective-permute-start) | collective-permute-done | bytes 786464 | tf_op jit(solution)/shard_map/ppermute | solution.py:12
  484.6 24.2 %conditional.3 = (bf16[512,6144]{1,0:T(8,128)(2,1)}) conditional(s32[]{:T(128)} %convert_element_type.36, (bf16[512,768]{1,0:T(8,128)(2,1)S(1)}, bf16[6144,768]{1,0:T(8,128)(2,1)}, bf16[512,768]{1,0:T(8,128)(2,1)S(1)}, bf16[6144,768]{1,0:T(8,128)(2,1)}) %tuple.21, (bf16[512,768]{0,1:T(8,128)(2,1)}, bf16[6144,768]{1,0:T(8,128)(2,1)}) %tuple.22), branch_computations={%region_5.6_spmd, %region_6.7_spmd} | conditional | flops 9669967872 | bytes 51904520 | solution.py:88
  484.6 11.6 %fusion.21 = f32[512,6144]{1,0:T(8,128)} fusion(bf16[512,768]{1,0:T(8,128)(2,1)S(1)} %get-tuple-element.38, bf16[6144,768]{1,0:T(8,128)(2,1)} %get-tuple-element.39), kind=kOutput, calls=%fused_computation.28 | convolution fusion | flops 4831838208 | bytes 22806528 | tf_op jit(solution)/shard_map/cond/branch_0_fun/dot_general | solution.py:57
  496.2 12.6 %convolution_add_fusion = bf16[512,6144]{1,0:T(8,128)(2,1)} fusion(f32[512,6144]{1,0:T(8,128)} %fusion.21, bf16[512,768]{1,0:T(8,128)(2,1)S(1)} %get-tuple-element.40, bf16[6144,768]{1,0:T(8,128)(2,1)} %get-tuple-element.41), kind=kOutput, calls=%fused_computation.23 | convolution fusion | flops 4838129664 | bytes 29097984 | tf_op jit(solution)/shard_map/cond/branch_0_fun/dot_general | solution.py:57
  508.8 0.0 reduce-scatter.2.cloned.1.call-update
  508.9 49.6 %reduce-scatter.2.cloned.1.call-done = bf16[512,768]{1,0:T(8,128)(2,1)} async-done(((bf16[512,6144]{1,0:T(8,128)(2,1)}), bf16[512,768]{1,0:T(8,128)(2,1)}) %reduce-scatter.2.cloned.1.call-update) | async-done | bytes 786448 | tf_op jit(solution)/shard_map/reduce_scatter | solution.py:93
Async XLA Ops:
  6.5 399.3 %all-gather.2.cloned.1.call-start = ((), (), s32[]{:S(2)}) async-start(), calls=%async_computation.1 | async-start | bytes 20054016 | tf_op jit(solution)/shard_map/all_gather | solution.py:64
  7.3 551.2 %reduce-scatter.2.cloned.1.call-start = ((), (), s32[]{:S(2)}) async-start(), calls=%async_computation.2 | async-start | bytes 7077888 | tf_op jit(solution)/shard_map/reduce_scatter | solution.py:93
  7.3 413.2 %copy-start.3 = (bf16[2,1,256,768]{3,2,1,0:T(8,128)(2,1)S(1)}, bf16[2,1,256,768]{3,2,1,0:T(8,128)(2,1)}, u32[]{:S(2)}) copy-start(bf16[2,1,256,768]{3,2,1,0:T(8,128)(2,1)} %param.13) | copy-start | bytes 2359300
  7.3 413.1 %copy-start.5 = (s32[2,1,256]{2,1,0:T(1,128)S(1)}, s32[2,1,256]{2,1,0:T(1,128)}, u32[]{:S(2)}) copy-start(s32[2,1,256]{2,1,0:T(1,128)} %param.14) | copy-start | bytes 6148
  422.1 45.7 %collective-permute-start.1 = (bf16[512,768]{1,0:T(8,128)(2,1)S(1)}, bf16[512,768]{1,0:T(8,128)(2,1)S(1)}, u32[]{:S(2)}, u32[]{:S(2)}) collective-permute-start(bf16[512,768]{1,0:T(8,128)(2,1)S(1)} %copy.40), channel_id=1, source_target_pairs={{128,0},{129,1},{130,2},{131,3},{132,4},{133,5},{134,6},{135,7},{1... | collective-permute-start | bytes 2359304 | tf_op jit(solution)/shard_map/ppermute | solution.py:12
  423.4 61.2 %collective-permute-start = (bf16[512,768]{1,0:T(8,128)(2,1)S(1)}, bf16[512,768]{1,0:T(8,128)(2,1)S(1)}, u32[]{:S(2)}, u32[]{:S(2)}) collective-permute-start(bf16[512,768]{1,0:T(8,128)(2,1)S(1)} %copy.39), channel_id=1, source_target_pairs={{128,0},{129,1},{130,2},{131,3},{132,4},{133,5},{134,6},{135,7},{1... | collective-permute-start | bytes 2359304 | tf_op jit(solution)/shard_map/ppermute | solution.py:12
Sparse Core Ops, SparseCore 0:
  9.1 396.7 all-gather.1
  509.0 49.4 reduce-scatter.1
where the time goes:
time: 565 us
  waiting for transfers between devices  509 us (90%)
  matrix products  24.2 us (4%)
  local copies, waits for them, and re-layouts  16.2 us (3%)
  between operations  13.5 us (2%)
    all_gather x1, waiting for transfers between devices, per_device(): gathered = lax.all_gather(weights, 'fsdp', axis=2, tiled=True)  399 us
    ppermute x2, waiting for transfers between devices, passed_along(): return lax.ppermute(value, axis, pairs)  59.9 us
    reduce_scatter x1, waiting for transfers between devices, per_device(): lax.psum_scatter(partial_sum.astype(jnp.bfloat16), 'segment', scatter_dim...  49.6 us
    dot_general x2, matrix products, project(): lax.dot_general(grad_rows, weight_cols, (((1,), (1,)), ((), ())), preferr...  24.2 us
    squeeze x1, local copies, waits for them, and re-layouts, per_device(): second_weight = gathered[0, 1]  14.6 us
  transfers between devices with their start and end apart: 4, of which 4 were waited for; matrix products, arithmetic and copies ran while one was open for 0% of the time, Pallas kernels for 0%

commit v1 on v0

--- a/solution.py
+++ b/solution.py
@@ -61,7 +61,8 @@
 
 def per_device(out_grad, queries, enc_keys, enc_values, key_mask, weights):
     decoder = lax.axis_index("section") == 1
-    gathered = lax.all_gather(weights, "fsdp", axis=2, tiled=True)
+    repeated = jnp.stack([weights] * lax.axis_size("fsdp"))
+    gathered = jnp.concatenate(lax.all_to_all(repeated, "fsdp", 0, 0), axis=2)
     first_weight = gathered[0, 0]
     second_weight = gathered[0, 1]
     micro_count, reaction_count, seq_length, feature_width = out_grad.shape

time: 565 us -> 608 us (1.076)
  waiting for transfers between devices: 509 us -> 532 us
  starting transfers between devices: 2.62 us -> 12.8 us
  local copies, waits for them, and re-layouts: 16.2 us -> 25.6 us
    all_to_all x0 -> x1, waiting for transfers between devices: none -> 431 us  [per_device(): gathered = jnp.concatenate(lax.all_to_all(repeated, 'fsdp', 0, 0), axis=2)]
    all_gather x1 -> x0, waiting for transfers between devices: 399 us -> none  [per_device(): gathered = lax.all_gather(weights, 'fsdp', axis=2, tiled=True)]
    all_to_all x0 -> x1, starting transfers between devices: none -> 10.2 us  [per_device(): gathered = jnp.concatenate(lax.all_to_all(repeated, 'fsdp', 0, 0), axis=2)]
    all_to_all x0 -> x1, local copies, waits for them, and re-layouts: none -> 9.76 us  [per_device(): gathered = jnp.concatenate(lax.all_to_all(repeated, 'fsdp', 0, 0), axis=2)]
    squeeze x1, local copies, waits for them, and re-layouts: 14.6 us -> 6.63 us  [per_device(): second_weight = gathered[0, 1]]
    reduce_scatter x1, waiting for transfers between devices: 49.6 us -> 41.7 us  [per_device(): lax.psum_scatter(partial_sum.astype(jnp.bfloat16), 'segment', scatter_dim...]
    another operation x3 -> x4, local copies, waits for them, and re-layouts: 1.04 us -> 8.69 us  [the longest x1 7.65 us: per_device(): repeated = jnp.stack([weights] * lax.axis_size('fsdp'))]
where the time goes in v1:
time: 608 us
  waiting for transfers between devices  532 us (88%)
  local copies, waits for them, and re-layouts  25.6 us (4%)
  matrix products  24.2 us (4%)
  between operations  13.5 us (2%)
  starting transfers between devices  12.8 us (2%)
    all_to_all x1, waiting for transfers between devices, per_device(): gathered = jnp.concatenate(lax.all_to_all(repeated, 'fsdp', 0, 0), axis=2)  431 us
    ppermute x2, waiting for transfers between devices, passed_along(): return lax.ppermute(value, axis, pairs)  59.6 us
    reduce_scatter x1, waiting for transfers between devices, per_device(): lax.psum_scatter(partial_sum.astype(jnp.bfloat16), 'segment', scatter_dim...  41.7 us
    dot_general x2, matrix products, project(): lax.dot_general(grad_rows, weight_cols, (((1,), (1,)), ((), ())), preferr...  24.2 us
  transfers between devices with their start and end apart: 4, of which 4 were waited for; matrix products, arithmetic and copies ran while one was open for 0% of the time, Pallas kernels for 0%

profile of v1, /device:TPU:1, one launch (start us, length us, event | category | flops | bytes accessed | tf_op | source)
XLA Modules:
  0.0 608.1 jit_solution(4045729082495823688)
XLA Ops:
  6.5 7.6 %stack.2 = bf16[16,1,2,384,768]{4,3,2,1,0:T(8,128)(2,1)} broadcast(bf16[2,384,768]{2,1,0:T(8,128)(2,1)} %bitcast.65), dimensions={2,3,4} | broadcast | bytes 20054016 | tf_op jit(solution)/shard_map/stack | solution.py:64
  14.2 10.2 %all-to-all-start = ((bf16[16,1,2,384,768]{4,3,2,1,0:T(8,128)(2,1)}), bf16[16,1,2,384,768]{4,3,2,1,0:T(8,128)(2,1)}, u32[]{:S(2)}, u32[]{:S(2)}) async-start(bf16[16,1,2,384,768]{4,3,2,1,0:T(8,128)(2,1)} %stack.2), calls=%async_computation | async-start | bytes 37748736 | tf_op jit(solution)/shard_map/all_to_all | solution.py:65
  24.4 0.0 reduce-scatter.2.cloned.1.call-start
  24.4 430.7 %all-to-all-done = bf16[16,1,2,384,768]{4,3,2,1,0:T(8,128)(2,1)} async-done(((bf16[16,1,2,384,768]{4,3,2,1,0:T(8,128)(2,1)}), bf16[16,1,2,384,768]{4,3,2,1,0:T(8,128)(2,1)}, u32[]{:S(2)}, u32[]{:S(2)}) %all-to-all-start) | async-done | bytes 18874400 | tf_op jit(solution)/shard_map/all_to_all | solution.py:65
  455.1 9.8 %copy.75 = bf16[16,1,2,384,768]{4,3,0,2,1:T(8,128)(2,1)S(1)} copy(bf16[16,1,2,384,768]{4,3,2,1,0:T(8,128)(2,1)} %all-to-all-done) | data formatting | bytes 37748736 | tf_op jit(solution)/shard_map/all_to_all | solution.py:65
  464.9 0.0 copy-start.3
  464.9 0.0 copy-start.5
  464.9 6.6 %slice_bitcast_fusion = (bf16[6144,768]{1,0:T(8,128)(2,1)}, bf16[6144,768]{1,0:T(8,128)(2,1)}) fusion(bf16[1,2,6144,768]{3,2,1,0:T(8,128)(2,1)S(1)} %bitcast.55), kind=kLoop, calls=%fused_computation.24 | loop fusion | bytes 37748736 | tf_op jit(solution)/shard_map/squeeze | solution.py:67
  471.5 0.0 copy-done.3
  471.5 0.0 copy-done.5
  471.5 1.1 conditional.2
  471.5 0.1 broadcast.24.clone.1
  471.6 0.1 broadcast.24.clone
  471.7 0.9 broadcast.24
  472.6 0.3 copy.80
  472.9 0.3 copy.81
  473.1 1.3 collective-permute-start.1
  474.4 1.3 collective-permute-start
  475.7 42.7 %collective-permute-done.1 = bf16[512,768]{1,0:T(8,128)(2,1)S(1)} collective-permute-done((bf16[512,768]{1,0:T(8,128)(2,1)S(1)}, bf16[512,768]{1,0:T(8,128)(2,1)S(1)}, u32[]{:S(2)}, u32[]{:S(2)}) %collective-permute-start.1) | collective-permute-done | bytes 786464 | tf_op jit(solution)/shard_map/ppermute | solution.py:12
  518.5 16.9 %collective-permute-done = bf16[512,768]{1,0:T(8,128)(2,1)S(1)} collective-permute-done((bf16[512,768]{1,0:T(8,128)(2,1)S(1)}, bf16[512,768]{1,0:T(8,128)(2,1)S(1)}, u32[]{:S(2)}, u32[]{:S(2)}) %collective-permute-start) | collective-permute-done | bytes 786464 | tf_op jit(solution)/shard_map/ppermute | solution.py:12
  535.3 24.2 %conditional.3 = (bf16[512,6144]{1,0:T(8,128)(2,1)}) conditional(s32[]{:T(128)} %convert_element_type.36, (bf16[512,768]{1,0:T(8,128)(2,1)S(1)}, bf16[6144,768]{1,0:T(8,128)(2,1)}, bf16[512,768]{1,0:T(8,128)(2,1)S(1)}, bf16[6144,768]{1,0:T(8,128)(2,1)}) %tuple.21, (bf16[512,768]{0,1:T(8,128)(2,1)}, bf16[6144,768]{1,0:T(8,128)(2,1)}) %tuple.22), branch_computations={%region_5.6_spmd, %region_6.7_spmd} | conditional | flops 9669967872 | bytes 51904520 | solution.py:89
  535.3 11.6 %fusion.21 = f32[512,6144]{1,0:T(8,128)} fusion(bf16[512,768]{1,0:T(8,128)(2,1)S(1)} %get-tuple-element.38, bf16[6144,768]{1,0:T(8,128)(2,1)} %get-tuple-element.39), kind=kOutput, calls=%fused_computation.28 | convolution fusion | flops 4831838208 | bytes 22806528 | tf_op jit(solution)/shard_map/cond/branch_0_fun/dot_general | solution.py:57
  546.9 12.6 %convolution_add_fusion = bf16[512,6144]{1,0:T(8,128)(2,1)} fusion(f32[512,6144]{1,0:T(8,128)} %fusion.21, bf16[512,768]{1,0:T(8,128)(2,1)S(1)} %get-tuple-element.40, bf16[6144,768]{1,0:T(8,128)(2,1)} %get-tuple-element.41), kind=kOutput, calls=%fused_computation.23 | convolution fusion | flops 4838129664 | bytes 29097984 | tf_op jit(solution)/shard_map/cond/branch_0_fun/dot_general | solution.py:57
  559.5 0.0 reduce-scatter.2.cloned.1.call-update
  559.5 41.7 %reduce-scatter.2.cloned.1.call-done = bf16[512,768]{1,0:T(8,128)(2,1)} async-done(((bf16[512,6144]{1,0:T(8,128)(2,1)}), bf16[512,768]{1,0:T(8,128)(2,1)}) %reduce-scatter.2.cloned.1.call-update) | async-done | bytes 786448 | tf_op jit(solution)/shard_map/reduce_scatter | solution.py:94
Async XLA Ops:
  14.2 440.9 %all-to-all-start = ((bf16[16,1,2,384,768]{4,3,2,1,0:T(8,128)(2,1)}), bf16[16,1,2,384,768]{4,3,2,1,0:T(8,128)(2,1)}, u32[]{:S(2)}, u32[]{:S(2)}) async-start(bf16[16,1,2,384,768]{4,3,2,1,0:T(8,128)(2,1)} %stack.2), calls=%async_computation | async-start | bytes 37748736 | tf_op jit(solution)/shard_map/all_to_all | solution.py:65
  24.4 576.9 %reduce-scatter.2.cloned.1.call-start = ((), (), s32[]{:S(2)}) async-start(), calls=%async_computation.2 | async-start | bytes 7077888 | tf_op jit(solution)/shard_map/reduce_scatter | solution.py:94
  464.9 6.7 %copy-start.3 = (bf16[2,1,256,768]{3,2,1,0:T(8,128)(2,1)S(1)}, bf16[2,1,256,768]{3,2,1,0:T(8,128)(2,1)}, u32[]{:S(2)}) copy-start(bf16[2,1,256,768]{3,2,1,0:T(8,128)(2,1)} %param.13) | copy-start | bytes 2359300
  464.9 6.7 %copy-start.5 = (s32[2,1,256]{2,1,0:T(1,128)S(1)}, s32[2,1,256]{2,1,0:T(1,128)}, u32[]{:S(2)}) copy-start(s32[2,1,256]{2,1,0:T(1,128)} %param.14) | copy-start | bytes 6148
  473.1 45.3 %collective-permute-start.1 = (bf16[512,768]{1,0:T(8,128)(2,1)S(1)}, bf16[512,768]{1,0:T(8,128)(2,1)S(1)}, u32[]{:S(2)}, u32[]{:S(2)}) collective-permute-start(bf16[512,768]{1,0:T(8,128)(2,1)S(1)} %copy.81), channel_id=1, source_target_pairs={{128,0},{129,1},{130,2},{131,3},{132,4},{133,5},{134,6},{135,7},{1... | collective-permute-start | bytes 2359304 | tf_op jit(solution)/shard_map/ppermute | solution.py:12
  474.4 60.9 %collective-permute-start = (bf16[512,768]{1,0:T(8,128)(2,1)S(1)}, bf16[512,768]{1,0:T(8,128)(2,1)S(1)}, u32[]{:S(2)}, u32[]{:S(2)}) collective-permute-start(bf16[512,768]{1,0:T(8,128)(2,1)S(1)} %copy.80), channel_id=1, source_target_pairs={{128,0},{129,1},{130,2},{131,3},{132,4},{133,5},{134,6},{135,7},{1... | collective-permute-start | bytes 2359304 | tf_op jit(solution)/shard_map/ppermute | solution.py:12
Sparse Core Ops, SparseCore 0:
  559.6 41.5 reduce-scatter.1
